TPU v7x, 32 devices: a whole 2x2x4 slice. The times are simulated.
32 devices in a mesh: seq: 16 (over z, x, core), head: 2 (over y).
Axes of the slice: x: 2, y: 2, z: 4, core: 2. Of those that a mesh axis runs over, the one named last changes fastest.
Arguments:
- features: bfloat16 [8, 32, 8, 512], P(None, 'seq', 'head'), may hold values from -540 to 540
- gn_gain: float32 [512], replicated, may hold values from 0.5 to 1.5
- gn_bias: float32 [512], replicated, may hold values from -3 to 3
- conv_weight: bfloat16 [3, 3, 3, 16, 512], replicated, may hold values from -0.0546875 to 0.0546875
- conv_bias: float32 [16], replicated, may hold values from -3 to 3
- patch_weight: bfloat16 [64, 3072], replicated, may hold values from -0.75 to 0.75
- patch_bias: float32 [3072], replicated, may hold values from -3 to 3
- image_mod: float32 [3, 3072], replicated, may hold values from -3 to 3
- w_qkv: bfloat16 [3072, 3, 2048], P('seq', None, 'head'), may hold values from -5 to 5
- text_ids: int32 [512], replicated, may hold values from 0 to 16383
- text_length: int32 [1], replicated, may hold values from 256 to 512
- text_table: bfloat16 [3072, 16384], P('seq'), may hold values from -60 to 60
- text_mod: float32 [2, 3072], P(None, 'seq'), may hold values from -3 to 3
- w_text: bfloat16 [3072, 2, 2048], P('seq', None, 'head'), may hold values from -2 to 2
- w_out: bfloat16 [2048, 3072], P('head'), may hold values from -0.625 to 0.625
- out_bias: float32 [3072], replicated, may hold values from -3 to 3
Outputs:
- block_out: bfloat16 [8, 16, 4, 3072], P(None, 'seq', 'head')
All inputs are finite; a program needn't handle non-finite values.
Results may differ from a plain program's by a relative error of at most 0.0089.
Values may be sent and summed in bfloat16 or wider, within the bound.
A program may use at most 128 MiB of HBM per device.

v0:
```python
import math
import jax
import jax.numpy as jnp
from jax import lax
from jax.sharding import PartitionSpec as P

HD = 128
GN_GROUPS = 32
eps_norm = 1e-06


def with_halo(cells, sides, width):
    for axis, dim in sides:
        count = lax.axis_size(axis)
        ends = count - 1
        head = lax.slice_in_dim(cells, 0, width, axis=dim)
        tail = lax.slice_in_dim(cells, cells.shape[dim] - width, cells.shape[dim], axis=dim)
        cells = jnp.concatenate(
            [
                lax.ppermute(tail, axis, [(i, (i + 1) % count) for i in range(ends)]),
                cells,
                lax.ppermute(head, axis, [((i + 1) % count, i) for i in range(ends)]),
            ],
            axis=dim,
        )
    return cells


def patchify(latent):
    frame_count, row_count, col_count, chan_count = latent.shape
    blocks = latent.reshape(frame_count, row_count // 2, 2, col_count // 2, 2, chan_count)
    blocks = blocks.transpose(0, 1, 3, 2, 4, 5)
    return blocks.reshape(frame_count * (row_count // 2) * (col_count // 2), 4 * chan_count)


def embed_tokens(patches, patch_weight, patch_bias, image_mod):
    hidden = jnp.dot(patches, patch_weight, preferred_element_type=jnp.float32) + patch_bias
    center = jnp.mean(hidden, axis=1, keepdims=True)
    offset = hidden - center
    spread = jnp.mean(offset * offset, axis=1, keepdims=True)
    normed = offset * lax.rsqrt(spread + eps_norm)
    modulated = (normed * (1.0 + image_mod[1]) + image_mod[0]).astype(jnp.bfloat16)
    return (hidden, modulated)


def text_start(query, text_keys, text_values, text_valid):
    scores = jnp.einsum("qhe,khe->qhk", query, text_keys, preferred_element_type=jnp.float32) / HD
    scores = jnp.where(text_valid[None, None, :], scores, -1e30)
    first_top = jnp.max(scores, axis=2)
    probs = jnp.exp(scores - first_top[..., None])
    first_total = jnp.sum(probs, axis=2)
    first_acc = jnp.einsum(
        "qhk,khe->qhe", probs.astype(jnp.bfloat16), text_values, preferred_element_type=jnp.float32
    )
    return (first_top, first_total, first_acc)


def attend_rows(query, state, piece):
    piece_rows = piece.shape[0]
    block_rows = math.gcd(piece_rows, 2048)
    heads_count = query.shape[1]
    blocks = piece.reshape(piece_rows // block_rows, block_rows, 2, heads_count, HD)

    def one_block(inner, block):
        run_top, run_total, run_acc = inner
        scores = (
            jnp.einsum("qhe,khe->qhk", query, block[:, 0], preferred_element_type=jnp.float32) / HD
        )
        new_top = jnp.maximum(run_top, jnp.max(scores, axis=2))
        factor = jnp.exp(run_top - new_top)
        probs = jnp.exp(scores - new_top[..., None])
        run_total = run_total * factor + jnp.sum(probs, axis=2)
        run_acc = run_acc * factor[..., None] + jnp.einsum(
            "qhk,khe->qhe",
            probs.astype(jnp.bfloat16),
            block[:, 1],
            preferred_element_type=jnp.float32,
        )
        return ((new_top, run_total, run_acc), None)

    return lax.scan(one_block, state, blocks)[0]


def body(
    features,
    gn_gain,
    gn_bias,
    conv_weight,
    conv_bias,
    patch_weight,
    patch_bias,
    image_mod,
    w_qkv,
    text_ids,
    text_length,
    text_table,
    text_mod,
    w_text,
    w_out,
    out_bias,
):
    frame_count, row_count, col_count, chan_count = features.shape
    width_full = patch_weight.shape[1]
    values = features.astype(jnp.float32)
    grouped = values.reshape(frame_count, row_count, col_count, GN_GROUPS, chan_count // GN_GROUPS)
    group_sums = jnp.sum(grouped, axis=(0, 1, 2, 4))
    group_squares = jnp.sum(grouped * grouped, axis=(0, 1, 2, 4))
    group_sums, group_squares = lax.psum((group_sums, group_squares), ("seq", "head"))
    cell_count = (
        frame_count
        * row_count
        * col_count
        * (chan_count // GN_GROUPS)
        * lax.axis_size("seq")
        * lax.axis_size("head")
    )
    group_mean = group_sums / cell_count
    group_scale = lax.rsqrt(group_squares / cell_count - group_mean * group_mean + eps_norm)
    normed = ((grouped - group_mean[:, None]) * group_scale[:, None]).reshape(
        frame_count, row_count, col_count, chan_count
    )
    activated = jax.nn.silu(normed * gn_gain + gn_bias).astype(jnp.bfloat16)
    rimmed = with_halo(activated, (("seq", 1), ("head", 2)), 1)
    padded = jnp.concatenate([rimmed[:1], rimmed[:1], rimmed], axis=0)
    windows = []
    for time_off in range(3):
        for row_off in range(3):
            for col_off in range(3):
                windows.append(
                    padded[
                        time_off : time_off + frame_count,
                        row_off : row_off + row_count,
                        col_off : col_off + col_count,
                    ]
                )
    stacked = jnp.stack(windows, axis=3)
    latent_chans = conv_weight.shape[3]
    kernels = conv_weight.reshape(27, latent_chans, chan_count)
    latent_sum = jnp.einsum("fyxkc,kzc->fyxz", stacked, kernels, preferred_element_type=jnp.float32)
    latent = (latent_sum + conv_bias).astype(jnp.bfloat16)
    patches = patchify(latent)
    hidden, own_modulated = embed_tokens(patches, patch_weight, patch_bias, image_mod)
    modulated = lax.all_gather(own_modulated, "head", axis=0, tiled=True)
    token_count = modulated.shape[0]
    head_width = w_qkv.shape[2]
    heads_here = head_width // HD
    qkv = jnp.einsum(
        "nd,dkj->nkj",
        modulated,
        lax.all_gather(w_qkv, "seq", axis=0, tiled=True),
        preferred_element_type=jnp.float32,
    ).astype(jnp.bfloat16)
    context = jnp.take(text_table, text_ids, axis=1).astype(jnp.float32)
    text_weight = w_text.astype(jnp.float32)
    text_gain = 1.0 + text_mod[1]
    text_shift = text_mod[0]
    text_sums, text_squares = lax.psum(
        (jnp.sum(context, axis=0), jnp.sum(context * context, axis=0)), "seq"
    )
    text_mean = text_sums / width_full
    text_scale = lax.rsqrt(text_squares / width_full - text_mean * text_mean + eps_norm)
    text_normed = (context - text_mean) * text_scale * text_gain[:, None] + text_shift[:, None]
    partial_kv = jnp.einsum(
        "dt,dkj->tkj", text_normed, text_weight, precision=lax.Precision.HIGHEST
    )
    text_kv = lax.psum(partial_kv, "seq")
    text_kv = text_kv.astype(jnp.bfloat16)
    text_count = text_kv.shape[0]
    text_valid = jnp.arange(text_count, dtype=jnp.int32) < text_length[0]
    query = qkv[:, 0].reshape(token_count, heads_here, HD)
    text_keys = text_kv[:, 0].reshape(text_count, heads_here, HD)
    text_values = text_kv[:, 1].reshape(text_count, heads_here, HD)
    first_state = text_start(query, text_keys, text_values, text_valid)
    image_kv = qkv[:, 1:3]
    run_top, run_total, run_acc = attend_rows(
        query, first_state, lax.all_gather(image_kv, "seq", axis=0, tiled=True)
    )
    attended = (
        (run_acc / run_total[..., None]).astype(jnp.bfloat16).reshape(token_count, head_width)
    )
    projected = (
        lax.psum_scatter(
            jnp.dot(attended, w_out, preferred_element_type=jnp.float32),
            "head",
            scatter_dimension=0,
            tiled=True,
        )
        + out_bias
    )
    block_out = (hidden + image_mod[2] * projected).astype(jnp.bfloat16)
    return block_out.reshape(frame_count, row_count // 2, col_count // 2, width_full)


def solution(mesh):
    return jax.shard_map(
        body,
        mesh=mesh,
        in_specs=(
            P(None, "seq", "head", None),
            P(),
            P(),
            P(),
            P(),
            P(),
            P(),
            P(),
            P("seq", None, "head"),
            P(),
            P(),
            P("seq", None),
            P(None, "seq"),
            P("seq", None, "head"),
            P("head", None),
            P(),
        ),
        out_specs=P(None, "seq", "head", None),
        check_vma=False,
    )
```

profile of v0, /device:TPU:0, one launch (start us, length us, event | category | flops | bytes accessed | tf_op | source)
XLA Modules:
  0.0 285.2 jit_solution(11076966553390359524)
XLA Ops:
  6.5 0.7 all-gather.3.cloned.1.call-update
  7.3 0.0 all-gather.5.cloned.1.call-start
  7.3 0.9 convert_reduce_fusion.1
  8.2 0.1 reduce_sum.88
  8.3 0.1 reduce_sum.91
  8.3 0.1 reduce_sum.89
  8.5 0.1 reduce_sum.92
  8.6 43.1 %all-reduce = (f32[32]{0:T(128)S(1)}, f32[32]{0:T(128)S(1)}) all-reduce(f32[32]{0:T(128)S(1)} %reduce_sum.92, f32[32]{0:T(128)S(1)} %reduce_sum.89), channel_id=1, replica_groups=mesh['seq'=16,'head'=2] {'seq','head'}, use_global_device_ids=true, to_apply=%region_5.6 | all-reduce | flops 64 | bytes 512 | tf_op jit(solution)/shard_map/psum | solution.py:108
  51.7 0.1 mul.107
  51.7 0.1 mul.108
  51.8 0.1 sub.66
  51.9 0.1 sub.67
  52.0 1.0 fusion.41
  52.9 1.8 collective-permute-start
  54.7 1.3 collective-permute-start.1
  56.0 0.7 compare_select_fusion
  56.7 1.0 fusion.78
  57.7 0.7 compare_and_fusion
  58.4 1.5 collective-permute-done.1
  59.9 2.5 collective-permute-start.2
  62.4 1.3 collective-permute-start.3
  63.7 10.1 %copy.82 = bf16[192,16384]{0,1:T(8,128)(2,1)} copy(bf16[192,16384]{1,0:T(8,128)(2,1)} %param.27) | data formatting | bytes 12582912 | tf_op args[11]
  73.8 6.2 %gather_fusion = bf16[512,192]{1,0:T(8,128)(2,1)S(1)} fusion(bf16[192,16384]{0,1:T(8,128)(2,1)} %copy.82, s32[1024]{0:T(1024)S(1)} %pad_clamp_fusion), kind=kCustom, calls=%fused_computation | custom fusion | bytes 395264 | tf_op jit(solution)/shard_map/jit(_take)/gather | solution.py:153
  80.1 0.2 maximum_maximum_fusion
  80.3 0.0 copy-start.1
  80.4 0.0 copy-start.7
  80.4 0.1 maximum_maximum_fusion.1
  80.5 0.0 copy-start.3
  80.5 0.0 copy-start.9
  80.9 0.3 copy-done.1
  81.2 0.1 bitcast_dynamic-update-slice_fusion
  81.3 0.2 copy-done.3
  81.6 0.6 fusion.9
  82.2 0.1 reshape.85
  82.3 0.3 fusion.79
  82.6 0.2 multiply_reduce_fusion
  82.8 0.1 add_convert_fusion.1
  82.9 5.9 %all_gather.9 = bf16[32,3072]{1,0:T(8,128)(2,1)S(1)} all-gather(bf16[16,3072]{1,0:T(8,128)(2,1)S(1)} %add_convert_fusion.1), channel_id=1, replica_groups=mesh['seq'=16,'head'=2] {'head'}, dimensions={0}, use_global_device_ids=true | all-gather | bytes 294912 | tf_op jit(solution)/shard_map/all_gather | solution.py:143
  88.8 23.2 %all-gather.3.cloned.1.call-done = bf16[3072,3,1024]{2,0,1:T(8,128)(2,1)} async-done(((bf16[192,3,1024]{2,0,1:T(8,128)(2,1)}), bf16[3072,3,1024]{2,0,1:T(8,128)(2,1)}) %all-gather.3.cloned.1.call-update) | async-done | bytes 18874384 | tf_op jit(solution)/shard_map/all_gather | solution.py:150
  112.0 9.7 %convolution_convert_fusion = bf16[32,3,1024]{2,0,1:T(8,128)(2,1)S(1)} fusion(bf16[3072,3,1024]{2,0,1:T(8,128)(2,1)} %all-gather.3.cloned.1.call-done, bf16[32,3072]{1,0:T(8,128)(2,1)S(1)} %all_gather.9), kind=kOutput, calls=%fused_computation.7 | convolution fusion | flops 604078080 | bytes 19267584 | tf_op jit(solution)/shard_map/nd,dkj->nkj/dot_general | solution.py:147
  121.7 0.7 slice.219
  122.3 0.0 all-gather.5.cloned.1.call-update
  122.4 0.0 reduce-scatter.2.cloned.1.call-start
  122.4 0.4 convert_reduce_fusion
  122.8 33.0 %all-reduce.1 = (f32[512]{0:T(512)S(1)}, f32[512]{0:T(512)S(1)}) all-reduce(f32[512]{0:T(512)S(1)} %get-tuple-element.16, f32[512]{0:T(512)S(1)} %get-tuple-element.15), channel_id=1, replica_groups=mesh['seq'=16,'head'=2] {'seq'}, use_global_device_ids=true, to_apply=%region_9.10 | all-reduce | flops 1024 | bytes 8192 | tf_op jit(solution)/shard_map/psum | solution.py:157
  155.8 3.9 %fusion.12 = f32[512,2,1024]{2,0,1:T(8,128)} fusion(bf16[192,2,1024]{2,1,0:T(2,128)(2,1)S(1)} %copy-done, f32[192]{0:T(256)S(1)} %bitcast.263, f32[192]{0:T(256)S(1)} %bitcast.262, f32[512]{0:T(512)S(1)} %get-tuple-element.47, f32[512]{0:T(512)S(1)} %get-tuple-element.46, bf16[512,192]{1,0:T(8,128)(2,1)S(1)} %gather_fusion, ...), kind=kOutput, calls=%fused_computation.24 | convolution fusion | flops 2416508928 | bytes 5183488 | tf_op jit(solution)/shard_map/dt,dkj->tkj/dot_general | solution.py:163
  159.7 94.6 %all-reduce.3 = bf16[512,2,1024]{2,0,1:T(8,128)(2,1)S(1)} all-reduce(f32[512,2,1024]{2,0,1:T(8,128)} %fusion.12), channel_id=1, replica_groups=mesh['seq'=16,'head'=2] {'seq'}, use_global_device_ids=true, to_apply=%region_10.11 | all-reduce | flops 1048576 | bytes 6291456 | tf_op jit(solution)/shard_map/psum | solution.py:166
  254.3 0.2 slice_bitcast_fusion
  254.5 0.3 copy.100
  255.4 0.3 copy.102
  255.8 1.3 fusion.80
  257.0 2.4 copy.103
  259.4 0.0 slice-start.1
  259.4 0.1 fusion.76
  259.6 0.6 fusion.81
  260.1 0.6 copy-done.2
  260.7 0.3 fusion.20
  261.1 0.4 convolution_bitcast_fusion
  261.5 0.4 fusion.7
  261.9 1.9 fusion.43
  263.9 0.0 reduce-scatter.2.cloned.1.call-update
  263.9 13.2 %reduce-scatter.2.cloned.1.call-done = f32[16,3072]{1,0:T(8,128)} async-done(((f32[32,3072]{1,0:T(8,128)}), f32[16,3072]{1,0:T(8,128)}) %reduce-scatter.2.cloned.1.call-update) | async-done | bytes 196624 | tf_op jit(solution)/shard_map/reduce_scatter | solution.py:182
  277.1 1.0 add_convert_fusion
  278.0 0.7 reshape.87
  (66 shorter events, 0.4 us)
Async XLA Ops:
  6.5 149.3 %copy-start = (bf16[192,2,1024]{2,1,0:T(2,128)(2,1)S(1)}, bf16[192,2,1024]{2,1,0:T(2,128)(2,1)}, u32[]{:S(2)}) copy-start(bf16[192,2,1024]{2,1,0:T(2,128)(2,1)} %param.29) | copy-start | bytes 2359300
  6.5 105.4 %all-gather.3.cloned.1.call-start = ((), (), s32[]{:S(2)}) async-start(), calls=%async_computation.1 | async-start | bytes 20054016 | tf_op jit(solution)/shard_map/all_gather | solution.py:150
  7.3 249.8 %all-gather.5.cloned.1.call-start = ((), (), s32[]{:S(2)}) async-start(), calls=%async_computation.2 | async-start | bytes 2228224 | tf_op jit(solution)/shard_map/all_gather | solution.py:176
  52.9 5.4 %collective-permute-start = (bf16[8,1,4,512]{3,0,2,1:T(8,128)(2,1)S(1)}, bf16[8,1,4,512]{3,0,2,1:T(8,128)(2,1)S(1)}, u32[]{:S(2)}, u32[]{:S(2)}) collective-permute-start(bf16[8,1,4,512]{3,0,2,1:T(8,128)(2,1)S(1)} %get-tuple-element.41), channel_id=1, source_target_pairs={{0,2},{2,4},{4,6},{6,8},{8,10},{10,12},{12,14},{14,16},{16,18},{18... | collective-permute-start | bytes 98312 | tf_op jit(solution)/shard_map/ppermute | solution.py:20
  54.7 5.2 %collective-permute-start.1 = (bf16[8,1,4,512]{3,0,2,1:T(8,128)(2,1)S(1)}, bf16[8,1,4,512]{3,0,2,1:T(8,128)(2,1)S(1)}, u32[]{:S(2)}, u32[]{:S(2)}) collective-permute-start(bf16[8,1,4,512]{3,0,2,1:T(8,128)(2,1)S(1)} %get-tuple-element.42), channel_id=1, source_target_pairs={{2,0},{4,2},{6,4},{8,6},{10,8},{12,10},{14,12},{16,14},{18,16},{20... | collective-permute-start | bytes 98312 | tf_op jit(solution)/shard_map/ppermute | solution.py:22
  59.9 20.1 %collective-permute-start.2 = (bf16[8,4,1,512]{3,0,2,1:T(8,128)(2,1)S(1)}, bf16[8,4,1,512]{3,0,2,1:T(8,128)(2,1)S(1)}, u32[]{:S(2)}, u32[]{:S(2)}) collective-permute-start(bf16[8,4,1,512]{3,0,2,1:T(8,128)(2,1)S(1)} %get-tuple-element.39), channel_id=1, source_target_pairs={{0,1},{2,3},{4,5},{6,7},{8,9},{10,11},{12,13},{14,15},{16,17},{18,... | collective-permute-start | bytes 98312 | tf_op jit(solution)/shard_map/ppermute | solution.py:20
  62.4 17.6 %collective-permute-start.3 = (bf16[8,4,1,512]{3,0,2,1:T(8,128)(2,1)S(1)}, bf16[8,4,1,512]{3,0,2,1:T(8,128)(2,1)S(1)}, u32[]{:S(2)}, u32[]{:S(2)}) collective-permute-start(bf16[8,4,1,512]{3,0,2,1:T(8,128)(2,1)S(1)} %get-tuple-element.40), channel_id=1, source_target_pairs={{1,0},{3,2},{5,4},{7,6},{9,8},{11,10},{13,12},{15,14},{17,16},{19,... | collective-permute-start | bytes 98312 | tf_op jit(solution)/shard_map/ppermute | solution.py:22
  80.3 0.8 copy-start.1
  80.4 0.8 copy-start.7
  80.4 0.8 copy-start.8
  80.5 1.0 copy-start.3
  80.5 1.0 copy-start.9
  80.8 1.5 copy-start.4
  80.8 1.5 copy-start.5
  88.8 67.0 %copy-start.10 = (f32[2,192]{1,0:T(2,128)S(1)}, f32[2,192]{1,0:T(2,128)}, u32[]{:S(2)}) copy-start(f32[2,192]{1,0:T(2,128)} %param.28) | copy-start | bytes 4612
  122.4 154.7 %reduce-scatter.2.cloned.1.call-start = ((), (), s32[]{:S(2)}) async-start(), calls=%async_computation.3 | async-start | bytes 589824 | tf_op jit(solution)/shard_map/reduce_scatter | solution.py:182
  257.0 4.9 %slice-start = ((s8[6291456]{0:T(1024)(128)(4,1)}), s8[4194304]{0:T(1024)(128)(4,1)S(1)}, s32[]{:S(2)}) async-start(s8[6291456]{0:T(1024)(128)(4,1)} %bitcast.249), calls=%async_computation.4 | async-start | bytes 8388608
  259.4 2.5 slice-start.1
  259.6 1.2 copy-start.2
  261.9 15.2 %copy-start.6 = (f32[3072]{0:T(1024)S(1)}, f32[3072]{0:T(1024)}, u32[]{:S(2)}) copy-start(f32[3072]{0:T(1024)} %param.31) | copy-start | bytes 36868
Sparse Core Ops, SparseCore 0:
  8.9 103.0 all-gather.2
  122.5 42.3 all-gather.4
  264.0 12.9 reduce-scatter.1
where the time goes:
time: 286 us; the launch traced here: 285 us
  blocking collectives  177 us (62%)
  waiting for transfers between devices  38.6 us (13%)
  local copies, waits for them, and re-layouts  22.7 us (8%)
  matrix products  19.1 us (7%)
  between operations  14.3 us (5%)
  starting transfers between devices  6.94 us (2%)
  other arithmetic  6.94 us (2%)
    psum x1, blocking collectives, body(): text_kv = lax.psum(partial_kv, 'seq')  94.6 us
    psum x1, blocking collectives, body(): lax.psum((group_sums, group_squares), ('seq', 'head'))  43.1 us
    psum x1, blocking collectives, body(): lax.psum((jnp.sum(context, axis=0), jnp.sum(context * context, axis=0)),...  33 us
    all_gather x1, waiting for transfers between devices, body(): lax.all_gather(w_qkv, 'seq', axis=0, tiled=True)  23.2 us
    unnamed x56, local copies, waits for them, and re-layouts  14.5 us
    reduce_scatter x1, waiting for transfers between devices, body(): lax.psum_scatter(jnp.dot(attended, w_out, preferred_element_type=jnp.floa...  13.2 us
    dot_general x1, matrix products, body(): jnp.einsum('nd,dkj->nkj', modulated, lax.all_gather(w_qkv, 'seq', axis=0,...  9.7 us
    gather x1, local copies, waits for them, and re-layouts, body(): context = jnp.take(text_table, text_ids, axis=1).astype(jnp.float32)  6.18 us
  transfers between devices with their start and end apart: 7, of which 3 were waited for; matrix products, arithmetic and copies ran while one was open for 10% of the time, Pallas kernels for 0%

commit v1 on v0

--- a/solution.py
+++ b/solution.py
@@ -105,7 +105,7 @@
     grouped = values.reshape(frame_count, row_count, col_count, GN_GROUPS, chan_count // GN_GROUPS)
     group_sums = jnp.sum(grouped, axis=(0, 1, 2, 4))
     group_squares = jnp.sum(grouped * grouped, axis=(0, 1, 2, 4))
-    group_sums, group_squares = lax.psum((group_sums, group_squares), ("seq", "head"))
+    group_sums, group_squares = lax.psum(lax.psum((group_sums, group_squares), "head"), "seq")
     cell_count = (
         frame_count
         * row_count

time: 286 us -> 306 us (1.070)
  waiting for transfers between devices: 38.6 us -> 57 us
  other arithmetic: 6.94 us -> 2.95 us
    all_gather x1, waiting for transfers between devices: 0.01 us -> 37.3 us  [body(): lax.all_gather(image_kv, 'seq', axis=0, tiled=True)]
    all_gather x1, waiting for transfers between devices: 23.2 us -> 0.01 us  [body(): lax.all_gather(w_qkv, 'seq', axis=0, tiled=True)]
    ppermute x2, waiting for transfers between devices: 1.55 us -> 6.64 us  [with_halo(): lax.ppermute(head, axis, [((i + 1) % count, i) for i in range(ends)])]
  transfers between devices with their start and end apart: 7 -> 7, of which waited for: 3 -> 5; matrix products, arithmetic and copies ran while one was open for 10% -> 9% of each run, Pallas kernels for 0% -> 0%
where the time goes in v1:
time: 306 us; the launch traced here: 305 us
  blocking collectives  179 us (58%)
  waiting for transfers between devices  57 us (19%)
  local copies, waits for them, and re-layouts  22.7 us (7%)
  matrix products  19.4 us (6%)
  between operations  14.4 us (5%)
  starting transfers between devices  10 us (3%)
    psum x1, blocking collectives, body(): lax.psum(lax.psum((group_sums, group_squares), 'head'), 'seq')  133 us
    all_gather x1, waiting for transfers between devices, body(): lax.all_gather(image_kv, 'seq', axis=0, tiled=True)  37.3 us
    psum x1, blocking collectives, body(): lax.psum((jnp.sum(context, axis=0), jnp.sum(context * context, axis=0)),...  35.2 us
    unnamed x56, local copies, waits for them, and re-layouts  13.8 us
    reduce_scatter x1, waiting for transfers between devices, body(): lax.psum_scatter(jnp.dot(attended, w_out, preferred_element_type=jnp.floa...  12 us
    dot_general x1, matrix products, body(): jnp.einsum('nd,dkj->nkj', modulated, lax.all_gather(w_qkv, 'seq', axis=0,...  9.7 us
    ppermute x2, starting transfers between devices, with_halo(): lax.ppermute(tail, axis, [(i, (i + 1) % count) for i in range(ends)])  7.19 us
    gather x1, local copies, waits for them, and re-layouts, body(): context = jnp.take(text_table, text_ids, axis=1).astype(jnp.float32)  6.8 us
  transfers between devices with their start and end apart: 7, of which 5 were waited for; matrix products, arithmetic and copies ran while one was open for 9% of the time, Pallas kernels for 0%

profile of v1, /device:TPU:0, one launch (start us, length us, event | category | flops | bytes accessed | tf_op | source)
XLA Modules:
  0.0 305.3 jit_solution(11119749072497073627)
XLA Ops:
  6.5 0.0 all-gather.3.cloned.1.call-start
  6.5 0.7 all-gather.3.cloned.1.call-update
  7.3 0.0 all-gather.5.cloned.1.call-start
  7.3 10.0 %copy.82 = bf16[192,16384]{0,1:T(8,128)(2,1)} copy(bf16[192,16384]{1,0:T(8,128)(2,1)} %param.27) | data formatting | bytes 12582912 | tf_op args[11]
  17.3 6.8 %gather_fusion = bf16[512,192]{1,0:T(8,128)(2,1)S(1)} fusion(bf16[192,16384]{0,1:T(8,128)(2,1)} %copy.82, s32[1024]{0:T(1024)S(1)} %pad_clamp_fusion), kind=kCustom, calls=%fused_computation | custom fusion | bytes 395264 | tf_op jit(solution)/shard_map/jit(_take)/gather | solution.py:153
  24.1 0.4 convert_reduce_fusion
  24.5 35.2 %all-reduce.1 = (f32[512]{0:T(512)S(1)}, f32[512]{0:T(512)S(1)}) all-reduce(f32[512]{0:T(512)S(1)} %get-tuple-element.16, f32[512]{0:T(512)S(1)} %get-tuple-element.15), channel_id=1, replica_groups=mesh['seq'=16,'head'=2] {'seq'}, use_global_device_ids=true, to_apply=%region_11.12 | all-reduce | flops 1024 | bytes 8192 | tf_op jit(solution)/shard_map/psum | solution.py:157
  59.7 0.0 copy-start.1
  59.7 4.0 %fusion.12 = f32[512,2,1024]{2,0,1:T(8,128)} fusion(bf16[192,2,1024]{2,1,0:T(2,128)(2,1)S(1)} %copy-done, f32[192]{0:T(256)S(1)} %bitcast.263, f32[192]{0:T(256)S(1)} %bitcast.262, f32[512]{0:T(512)S(1)} %get-tuple-element.50, f32[512]{0:T(512)S(1)} %get-tuple-element.49, bf16[512,192]{1,0:T(8,128)(2,1)S(1)} %gather_fusion, ...), kind=kOutput, calls=%fused_computation.24 | convolution fusion | flops 2416508928 | bytes 5183488 | tf_op jit(solution)/shard_map/dt,dkj->tkj/dot_general | solution.py:163
  63.7 0.1 reduce_sum.88
  63.8 0.1 reduce_sum.91
  63.9 0.1 reduce_sum.89
  64.0 0.1 reduce_sum.92
  64.1 4.9 %all-reduce.2 = (f32[32]{0:T(128)S(1)}, f32[32]{0:T(128)S(1)}) all-reduce(f32[32]{0:T(128)S(1)} %reduce_sum.92, f32[32]{0:T(128)S(1)} %reduce_sum.89), channel_id=1, replica_groups=mesh['seq'=16,'head'=2] {'head'}, use_global_device_ids=true, to_apply=%region_6.7 | all-reduce | flops 64 | bytes 512 | tf_op jit(solution)/shard_map/psum | solution.py:108
  69.1 132.7 %all-reduce.4 = (f32[32]{0:T(128)S(1)}, f32[32]{0:T(128)S(1)}, bf16[512,2,1024]{2,0,1:T(8,128)(2,1)S(1)}) all-reduce(f32[32]{0:T(128)S(1)} %get-tuple-element.32, f32[32]{0:T(128)S(1)} %get-tuple-element.33, f32[512,2,1024]{2,0,1:T(8,128)} %fusion.12), channel_id=1, replica_groups=mesh['seq'=16,'head'=2] {'seq'}, use_global_device_ids=true, to_apply=%region_7.8 | all-reduce | flops 1048640 | bytes 6291968 | tf_op jit(solution)/shard_map/psum | solution.py:108
  201.8 0.1 mul.107
  201.9 0.1 mul.108
  202.0 0.1 sub.66
  202.0 0.1 sub.67
  202.1 0.0 copy-done.7
  202.1 0.1 fusion.41
  202.2 3.8 %collective-permute-start = (bf16[8,1,4,512]{3,0,2,1:T(8,128)(2,1)S(1)}, bf16[8,1,4,512]{3,0,2,1:T(8,128)(2,1)S(1)}, u32[]{:S(2)}, u32[]{:S(2)}) collective-permute-start(bf16[8,1,4,512]{3,0,2,1:T(8,128)(2,1)S(1)} %get-tuple-element.44), channel_id=1, source_target_pairs={{0,2},{2,4},{4,6},{6,8},{8,10},{10,12},{12,14},{14,16},{16,18},{18... | collective-permute-start | bytes 98312 | tf_op jit(solution)/shard_map/ppermute | solution.py:20
  206.0 1.3 collective-permute-start.1
  207.3 0.0 collective-permute-done
  207.3 2.4 collective-permute-done.1
  209.8 3.4 %collective-permute-start.2 = (bf16[8,4,1,512]{3,0,2,1:T(8,128)(2,1)S(1)}, bf16[8,4,1,512]{3,0,2,1:T(8,128)(2,1)S(1)}, u32[]{:S(2)}, u32[]{:S(2)}) collective-permute-start(bf16[8,4,1,512]{3,0,2,1:T(8,128)(2,1)S(1)} %get-tuple-element.42), channel_id=1, source_target_pairs={{0,1},{2,3},{4,5},{6,7},{8,9},{10,11},{12,13},{14,15},{16,17},{18,... | collective-permute-start | bytes 98312 | tf_op jit(solution)/shard_map/ppermute | solution.py:20
  213.2 1.3 collective-permute-start.3
  214.5 0.2 collective-permute-done.2
  214.8 4.2 %collective-permute-done.3 = bf16[8,4,1,512]{3,0,2,1:T(8,128)(2,1)S(1)} collective-permute-done((bf16[8,4,1,512]{3,0,2,1:T(8,128)(2,1)S(1)}, bf16[8,4,1,512]{3,0,2,1:T(8,128)(2,1)S(1)}, u32[]{:S(2)}, u32[]{:S(2)}) %collective-permute-start.3) | collective-permute-done | bytes 32800 | tf_op jit(solution)/shard_map/ppermute | solution.py:22
  219.1 0.1 maximum_maximum_fusion.1
  219.2 0.2 maximum_maximum_fusion
  219.5 0.0 copy-start.2
  219.5 0.0 copy-start.9
  219.7 0.0 copy-start.4
  219.8 0.1 bitcast_dynamic-update-slice_fusion
  219.9 0.5 copy-done.2
  220.5 0.6 fusion.9
  221.1 0.1 reshape.85
  221.2 1.3 fusion.79
  222.5 0.2 multiply_reduce_fusion
  222.7 0.1 add_convert_fusion.1
  222.8 6.1 %all_gather.9 = bf16[32,3072]{1,0:T(8,128)(2,1)S(1)} all-gather(bf16[16,3072]{1,0:T(8,128)(2,1)S(1)} %add_convert_fusion.1), channel_id=1, replica_groups=mesh['seq'=16,'head'=2] {'head'}, dimensions={0}, use_global_device_ids=true | all-gather | bytes 294912 | tf_op jit(solution)/shard_map/all_gather | solution.py:143
  228.9 9.7 %convolution_convert_fusion = bf16[32,3,1024]{2,0,1:T(8,128)(2,1)S(1)} fusion(bf16[3072,3,1024]{2,0,1:T(8,128)(2,1)} %all-gather.3.cloned.1.call-done, bf16[32,3072]{1,0:T(8,128)(2,1)S(1)} %all_gather.9), kind=kOutput, calls=%fused_computation.7 | convolution fusion | flops 604078080 | bytes 19267584 | tf_op jit(solution)/shard_map/nd,dkj->nkj/dot_general | solution.py:147
  238.6 0.7 slice.219
  239.3 0.0 all-gather.5.cloned.1.call-update
  239.3 0.2 reduce-scatter.2.cloned.1.call-start
  239.6 0.2 slice_bitcast_fusion
  239.7 0.3 copy.100
  240.7 0.3 copy.102
  241.0 0.6 fusion.80
  241.6 37.3 %all-gather.5.cloned.1.call-done = bf16[512,2,1024]{2,0,1:T(8,128)(2,1)} async-done(((bf16[32,2,1024]{2,0,1:T(8,128)(2,1)}), bf16[512,2,1024]{2,0,1:T(8,128)(2,1)}) %all-gather.5.cloned.1.call-update) | async-done | bytes 2097168 | tf_op jit(solution)/shard_map/all_gather | solution.py:176
  278.9 2.4 copy.103
  281.2 0.0 slice-start.1
  281.3 0.1 fusion.76
  281.4 0.6 fusion.81
  282.0 0.3 fusion.20
  282.3 0.4 convolution_bitcast_fusion
  282.7 0.4 fusion.7
  283.2 0.0 copy-start.5
  283.2 1.9 fusion.43
  285.1 0.0 reduce-scatter.2.cloned.1.call-update
  285.1 12.0 %reduce-scatter.2.cloned.1.call-done = f32[16,3072]{1,0:T(8,128)} async-done(((f32[32,3072]{1,0:T(8,128)}), f32[16,3072]{1,0:T(8,128)}) %reduce-scatter.2.cloned.1.call-update) | async-done | bytes 196624 | tf_op jit(solution)/shard_map/reduce_scatter | solution.py:182
  297.2 1.0 add_convert_fusion
  298.1 0.7 reshape.87
  (66 shorter events, 0.5 us)
Async XLA Ops:
  6.5 53.1 %copy-start = (bf16[192,2,1024]{2,1,0:T(2,128)(2,1)S(1)}, bf16[192,2,1024]{2,1,0:T(2,128)(2,1)}, u32[]{:S(2)}) copy-start(bf16[192,2,1024]{2,1,0:T(2,128)(2,1)} %param.29) | copy-start | bytes 2359300
  6.5 222.4 %all-gather.3.cloned.1.call-start = ((), (), s32[]{:S(2)}) async-start(), calls=%async_computation.1 | async-start | bytes 20054016 | tf_op jit(solution)/shard_map/all_gather | solution.py:150
  7.3 10.0 %copy-start.8 = (s32[512]{0:T(512)S(1)}, s32[512]{0:T(512)}, u32[]{:S(2)}) copy-start(s32[512]{0:T(512)} %param.25) | copy-start | bytes 6148
  7.3 271.6 %all-gather.5.cloned.1.call-start = ((), (), s32[]{:S(2)}) async-start(), calls=%async_computation.2 | async-start | bytes 2228224 | tf_op jit(solution)/shard_map/all_gather | solution.py:176
  17.3 42.4 %copy-start.10 = (f32[2,192]{1,0:T(2,128)S(1)}, f32[2,192]{1,0:T(2,128)}, u32[]{:S(2)}) copy-start(f32[2,192]{1,0:T(2,128)} %param.28) | copy-start | bytes 4612
  59.7 4.0 %copy-start.1 = (bf16[8,2,4,512]{3,2,1,0:T(4,128)(2,1)S(1)}, bf16[8,2,4,512]{3,2,1,0:T(4,128)(2,1)}, u32[]{:S(2)}) copy-start(bf16[8,2,4,512]{3,2,1,0:T(4,128)(2,1)} %param.16) | copy-start | bytes 196612
  69.0 133.1 %copy-start.6 = (f32[512]{0:T(512)S(1)}, f32[512]{0:T(512)}, u32[]{:S(2)}) copy-start(f32[512]{0:T(512)} %param.18) | copy-start | bytes 6148
  69.1 133.1 %copy-start.7 = (f32[512]{0:T(512)S(1)}, f32[512]{0:T(512)}, u32[]{:S(2)}) copy-start(f32[512]{0:T(512)} %param.17) | copy-start | bytes 6148
  69.1 145.4 %copy-start.3 = (f32[3,3072]{1,0:T(4,128)S(1)}, f32[3,3072]{1,0:T(4,128)}, u32[]{:S(2)}) copy-start(f32[3,3072]{1,0:T(4,128)} %param.23) | copy-start | bytes 110596
  202.2 5.1 %collective-permute-start = (bf16[8,1,4,512]{3,0,2,1:T(8,128)(2,1)S(1)}, bf16[8,1,4,512]{3,0,2,1:T(8,128)(2,1)S(1)}, u32[]{:S(2)}, u32[]{:S(2)}) collective-permute-start(bf16[8,1,4,512]{3,0,2,1:T(8,128)(2,1)S(1)} %get-tuple-element.44), channel_id=1, source_target_pairs={{0,2},{2,4},{4,6},{6,8},{8,10},{10,12},{12,14},{14,16},{16,18},{18... | collective-permute-start | bytes 98312 | tf_op jit(solution)/shard_map/ppermute | solution.py:20
  206.0 3.7 %collective-permute-start.1 = (bf16[8,1,4,512]{3,0,2,1:T(8,128)(2,1)S(1)}, bf16[8,1,4,512]{3,0,2,1:T(8,128)(2,1)S(1)}, u32[]{:S(2)}, u32[]{:S(2)}) collective-permute-start(bf16[8,1,4,512]{3,0,2,1:T(8,128)(2,1)S(1)} %get-tuple-element.45), channel_id=1, source_target_pairs={{2,0},{4,2},{6,4},{8,6},{10,8},{12,10},{14,12},{16,14},{18,16},{20... | collective-permute-start | bytes 98312 | tf_op jit(solution)/shard_map/ppermute | solution.py:22
  209.8 5.0 %collective-permute-start.2 = (bf16[8,4,1,512]{3,0,2,1:T(8,128)(2,1)S(1)}, bf16[8,4,1,512]{3,0,2,1:T(8,128)(2,1)S(1)}, u32[]{:S(2)}, u32[]{:S(2)}) collective-permute-start(bf16[8,4,1,512]{3,0,2,1:T(8,128)(2,1)S(1)} %get-tuple-element.42), channel_id=1, source_target_pairs={{0,1},{2,3},{4,5},{6,7},{8,9},{10,11},{12,13},{14,15},{16,17},{18,... | collective-permute-start | bytes 98312 | tf_op jit(solution)/shard_map/ppermute | solution.py:20
  213.2 5.8 %collective-permute-start.3 = (bf16[8,4,1,512]{3,0,2,1:T(8,128)(2,1)S(1)}, bf16[8,4,1,512]{3,0,2,1:T(8,128)(2,1)S(1)}, u32[]{:S(2)}, u32[]{:S(2)}) collective-permute-start(bf16[8,4,1,512]{3,0,2,1:T(8,128)(2,1)S(1)} %get-tuple-element.43), channel_id=1, source_target_pairs={{1,0},{3,2},{5,4},{7,6},{9,8},{11,10},{13,12},{15,14},{17,16},{19,... | collective-permute-start | bytes 98312 | tf_op jit(solution)/shard_map/ppermute | solution.py:22
  219.5 1.0 copy-start.2
  219.5 1.0 copy-start.9
  219.7 1.5 copy-start.4
  239.3 57.8 %reduce-scatter.2.cloned.1.call-start = ((), (), s32[]{:S(2)}) async-start(), calls=%async_computation.3 | async-start | bytes 589824 | tf_op jit(solution)/shard_map/reduce_scatter | solution.py:182
  278.9 4.3 %slice-start = ((s8[6291456]{0:T(1024)(128)(4,1)}), s8[4194304]{0:T(1024)(128)(4,1)S(1)}, s32[]{:S(2)}) async-start(s8[6291456]{0:T(1024)(128)(4,1)} %bitcast.249), calls=%async_computation.4 | async-start | bytes 8388608
  281.2 1.9 slice-start.1
  283.2 14.0 %copy-start.5 = (f32[3072]{0:T(1024)S(1)}, f32[3072]{0:T(1024)}, u32[]{:S(2)}) copy-start(f32[3072]{0:T(1024)} %param.31) | copy-start | bytes 36868
Sparse Core Ops, SparseCore 0:
  8.9 142.0 all-gather.2
  239.4 39.3 all-gather.4
  285.2 11.8 reduce-scatter.1
